TPU v7x, 32 devices: a whole 2x2x4 slice. The times are simulated.
32 devices in a mesh: group: 2 (over y), tm: 4 (over z), tensor: 2 (over x), dp: 2 (over core).
Axes of the slice: x: 2, y: 2, z: 4, core: 2. Of those that a mesh axis runs over, the one named last changes fastest.
Arguments:
- frames_in: bfloat16 [4, 3072, 1024], P(('group', 'dp'), 'tm', 'tensor'), parts along dimension 0, may hold values from -6 to 6
- in_proj: bfloat16 [2, 1024, 1024], P(None, None, 'tensor'), may hold values from -0.1875 to 0.1875
- log_rates: float32 [8, 8], P(None, 'tensor'), as said below
- angles: float32 [8, 8], P(None, 'tensor'), may hold values from -3.140625 to 3.140625
- residues: float32 [2, 8, 1024], P(None, None, 'tensor'), may hold values from -3 to 3
- skip_gain: float32 [1024], P('tensor'), may hold values from -3 to 3
- lengths: int32 [4, 4], P(('group', 'dp')), parts along dimension 0, may hold values from 1 to 1536, 3072 in all within a row
- grad_out: bfloat16 [4, 3072, 1024], P(('group', 'dp'), 'tm', 'tensor'), parts along dimension 0, may hold values from -6 to 6
Outputs:
- mixed: bfloat16 [4, 3072, 1024], P(('group', 'dp'), 'tm', 'tensor'), parts along dimension 0
- input_grad: bfloat16 [4, 3072, 1024], P(('group', 'dp'), 'tm', 'tensor'), parts along dimension 0
- proj_grad: float32 [4, 1024, 1024], P('group', None, 'tensor'), parts along dimension 0
- residue_grad: float32 [4, 8, 1024], P('group', None, 'tensor'), parts along dimension 0
- skip_grad: float32 [2048], P(('group', 'tensor')), parts along dimension 0
There are 2 independent parts, one for each index of `group`. A program takes and returns all parts, laid end to end along the dimension named above; an argument that names none is the same for every part. Nothing has to cross between parts.
Inputs may be any that keep to these rules, and one draw needn't show every extreme that they name: Each clip has at least one frame; the lengths of a stream sum to 3072. `log_rates`: each entry lies between the logarithms of 0.1 / 3072 and 0.08.
All inputs are finite; a program needn't handle non-finite values.
Results may differ from a plain program's by a relative error of at most 0.0058.
Values may be sent and summed in bfloat16 or wider, within the bound.
A program may use at most 128 MiB of HBM per device.

v0:
```python
import math
import jax
import jax.numpy as jnp
from jax import lax
from jax.sharding import PartitionSpec as P

BLOCK_LEN = 128


def carried_in(value, axis, join, neutral, backward):
    count, mine = (lax.axis_size(axis), lax.axis_index(axis))
    pieces = jax.tree.map(lambda part: lax.all_gather(part, axis), value)
    if backward:
        pieces = jax.tree.map(lambda part: part[::-1], pieces)
        mine = count - 1 - mine
    total = jax.tree.map(
        lambda part, zero: jnp.full_like(part, 0) + jnp.asarray(zero, part.dtype), value, neutral
    )

    def lap(position, total):
        longer = join(total, jax.tree.map(lambda part: part[position], pieces))
        return jax.tree.map(lambda new, old: jnp.where(position < mine, new, old), longer, total)

    return lax.fori_loop(0, count - 1, lap, total)


def compose(earlier_map, later_map):
    early_re, early_im, early_sre, early_sim = earlier_map
    late_re, late_im, late_sre, late_sim = later_map
    return (
        late_re * early_re - late_im * early_im,
        late_re * early_im + late_im * early_re,
        late_re[..., None] * early_sre - late_im[..., None] * early_sim + late_sre,
        late_re[..., None] * early_sim + late_im[..., None] * early_sre + late_sim,
    )


def shards(frames_in, in_proj, log_rates, angles, residues, skip_gain, lengths, grad_out):
    rows_dev = frames_in.shape[1]
    channels = frames_in.shape[2]
    modes_dev, heads_dev = log_rates.shape
    head_width = channels // heads_dev
    block_count = rows_dev // BLOCK_LEN
    largest_value = lax.Precision.HIGHEST
    features = lax.all_gather(frames_in, "tensor", axis=2, tiled=True)[0]
    projected = jnp.einsum("ld,kdc->klc", features, in_proj, preferred_element_type=jnp.float32)
    query_rows = projected[0].astype(jnp.bfloat16)
    signal = projected[1].astype(jnp.bfloat16)
    decay_rate = jnp.exp(log_rates)
    weight = jnp.sqrt(-jnp.expm1(-2.0 * decay_rate))
    later_idx = lax.broadcasted_iota(jnp.int32, (BLOCK_LEN, BLOCK_LEN), 0)
    earlier_idx = lax.broadcasted_iota(jnp.int32, (BLOCK_LEN, BLOCK_LEN), 1)
    causal = later_idx >= earlier_idx
    lag_steps = jnp.maximum(later_idx - earlier_idx, 0).astype(jnp.float32)
    damping = jnp.where(causal, jnp.exp(-decay_rate[:, :, None, None] * lag_steps), 0.0)
    kern_re = damping * jnp.cos(angles[:, :, None, None] * lag_steps)
    kern_im = damping * jnp.sin(angles[:, :, None, None] * lag_steps)
    exponents = jnp.arange(1, rows_dev + 1, dtype=jnp.int32).astype(jnp.float32)
    exponent_real = jnp.exp(-decay_rate[:, :, None] * exponents) * jnp.cos(
        angles[:, :, None] * exponents
    )
    exponent_imaginary = jnp.exp(-decay_rate[:, :, None] * exponents) * jnp.sin(
        angles[:, :, None] * exponents
    )
    block_re = exponent_real[:, :, :BLOCK_LEN]
    block_im = exponent_imaginary[:, :, :BLOCK_LEN]
    clip_start = jnp.cumsum(lengths[0]) - lengths[0]
    first_frame = lax.axis_index("tm") * rows_dev
    frame_ids = first_frame + jnp.arange(rows_dev, dtype=jnp.int32)
    segment = jnp.sum((frame_ids[:, None] >= clip_start[None, :]).astype(jnp.int32), axis=1) - 1
    segment_before = jnp.sum((first_frame - 1 >= clip_start).astype(jnp.int32)) - 1
    seg_blocks = segment.reshape(block_count, BLOCK_LEN)
    seg_prior = jnp.concatenate([segment_before[None], seg_blocks[:-1, -1]])
    alive_dev = (segment == segment_before).astype(jnp.float32)
    carry_re = exponent_real[:, :, -1] * alive_dev[-1]
    carry_im = exponent_imaginary[:, :, -1] * alive_dev[-1]

    def split_coeffs(coeffs):
        coefficient_real = coeffs[0].reshape(modes_dev, heads_dev, head_width) * weight[:, :, None]
        coefficient_imaginary = (
            coeffs[1].reshape(modes_dev, heads_dev, head_width) * weight[:, :, None]
        )
        return (coefficient_real, coefficient_imaginary)

    def intra(signal32, coeffs, skip_vec):
        coefficient_real, coefficient_imaginary = split_coeffs(coeffs)
        skip_row = skip_vec.reshape(heads_dev, head_width)

        def block_step(carried, element):
            state_re, state_im = carried
            block_in, block_seg, prior_seg = element
            same_clip = (block_seg[:, None] == block_seg[None, :]).astype(jnp.float32)
            alive_mask = (block_seg == prior_seg).astype(jnp.float32)[None, None, :, None]
            inner_re = jnp.einsum(
                "mhts,shd->mhtd", kern_re * same_clip, block_in, precision=largest_value
            )
            inner_im = jnp.einsum(
                "mhts,shd->mhtd", kern_im * same_clip, block_in, precision=largest_value
            )
            aggregate_real = inner_re + alive_mask * (
                block_re[..., None] * state_re[:, :, None, :]
                - block_im[..., None] * state_im[:, :, None, :]
            )
            aggregate_imaginary = inner_im + alive_mask * (
                block_re[..., None] * state_im[:, :, None, :]
                + block_im[..., None] * state_re[:, :, None, :]
            )
            output = (
                skip_row * block_in
                + jnp.einsum(
                    "ywo,ywlo->lwo", coefficient_real, aggregate_real, precision=largest_value
                )
                - jnp.einsum(
                    "ywo,ywlo->lwo",
                    coefficient_imaginary,
                    aggregate_imaginary,
                    precision=largest_value,
                )
            )
            return ((aggregate_real[:, :, -1, :], aggregate_imaginary[:, :, -1, :]), output)

        initial = jnp.zeros((modes_dev, heads_dev, head_width), jnp.float32)
        blocks_in = signal32.reshape(block_count, BLOCK_LEN, heads_dev, head_width)
        final_state, outputs = lax.scan(
            jax.checkpoint(block_step), (initial, initial), (blocks_in, seg_blocks, seg_prior)
        )
        return (outputs.reshape(rows_dev, heads_dev, head_width), final_state)

    def carry_part(coeffs, enter_re, enter_im):
        coefficient_real, coefficient_imaginary = split_coeffs(coeffs)
        blended_real = coefficient_real * enter_re - coefficient_imaginary * enter_im
        blended_imaginary = coefficient_real * enter_im + coefficient_imaginary * enter_re
        carried_contribution = jnp.einsum(
            "zan,zas->nas", exponent_real, blended_real, precision=largest_value
        ) - jnp.einsum(
            "zan,zas->nas", exponent_imaginary, blended_imaginary, precision=largest_value
        )
        carried_contribution = carried_contribution * alive_dev[:, None, None]
        leave_re = carry_re[:, :, None] * enter_re - carry_im[:, :, None] * enter_im
        leave_im = carry_re[:, :, None] * enter_im + carry_im[:, :, None] * enter_re
        return (carried_contribution, (leave_re, leave_im))

    signal32 = signal.astype(jnp.float32)
    (local_out, local_end), pull_local = jax.vjp(intra, signal32, residues, skip_gain)
    identity = (
        jnp.ones_like(carry_re),
        jnp.zeros_like(carry_re),
        jnp.zeros_like(local_end[0]),
        jnp.zeros_like(local_end[0]),
    )
    entering = carried_in(
        (carry_re, carry_im, local_end[0], local_end[1]), "tm", compose, identity, False
    )
    enter_re, enter_im = (entering[2], entering[3])
    carry_result, pull_carry = jax.vjp(carry_part, residues, enter_re, enter_im)
    long_out = (local_out + carry_result[0]).reshape(rows_dev, channels)
    query32 = query_rows.astype(jnp.float32)
    upstream = grad_out[0].astype(jnp.float32)
    mixed = (query32 * long_out).astype(jnp.bfloat16)
    grad_long = (upstream * query32).reshape(rows_dev, heads_dev, head_width)
    grad_query = (upstream * long_out).astype(jnp.bfloat16)
    zero_state = jnp.zeros_like(enter_re)
    _, adjoint_re, adjoint_im = pull_carry((grad_long, (zero_state, zero_state)))
    leaving = carried_in(
        (carry_re, -carry_im, adjoint_re, adjoint_im), "tm", compose, identity, True
    )
    end_re, end_im = (leaving[2], leaving[3])
    coeff_carry, _, _ = pull_carry((grad_long, (end_re, end_im)))
    grad_signal, coeff_local, skip_local = pull_local((grad_long, (end_re, end_im)))
    grad_value = grad_signal.astype(jnp.bfloat16)
    stacked = jnp.stack([grad_query, grad_value])
    partial_in = jnp.einsum("klc,kdc->ld", stacked, in_proj, preferred_element_type=jnp.float32)
    input_grad = lax.psum_scatter(
        partial_in[None], "tensor", scatter_dimension=2, tiled=True
    ).astype(jnp.bfloat16)
    norm_scale = 1.0 / math.sqrt(rows_dev * lax.axis_size("tm") * lax.axis_size("dp"))
    proj_term = (
        jnp.einsum("ld,klc->kdc", features, stacked, preferred_element_type=jnp.float32)
        * norm_scale
    )
    coeff_term = (coeff_local + coeff_carry) * norm_scale
    skip_term = skip_local * norm_scale
    proj_sum, coeff_sum, skip_sum = lax.psum((proj_term, coeff_term, skip_term), ("tm", "dp"))
    return (mixed[None], input_grad, proj_sum, coeff_sum, skip_sum)


def solution(mesh):
    in_specs = (
        P(("group", "dp"), "tm", "tensor"),
        P(None, None, "tensor"),
        P(None, "tensor"),
        P(None, "tensor"),
        P(None, None, "tensor"),
        P("tensor"),
        P(("group", "dp"), None),
        P(("group", "dp"), "tm", "tensor"),
    )
    out_specs = (
        P(("group", "dp"), "tm", "tensor"),
        P(("group", "dp"), "tm", "tensor"),
        P("group", None, "tensor"),
        P("group", None, "tensor"),
        P(("group", "tensor")),
    )
    return jax.shard_map(shards, mesh=mesh, in_specs=in_specs, out_specs=out_specs, check_vma=False)
```

profile of v0, /device:TPU:0, one launch (start us, length us, event | category | flops | bytes accessed | tf_op | source)
XLA Modules:
  0.0 767.0 jit_solution(7219482252016499978)
XLA Ops:
  13.0 14.9 %all-gather = f32[32,4,1]{2,0,1:T(8,128)S(1)} all-gather(f32[8,4,1]{2,0,1:T(8,128)S(1)} %get-tuple-element.1668), channel_id=2, replica_groups=mesh['group'=2,'tm'=4,'tensor'=2,'dp'=2] {'tm'}, dimensions={0}, use_global_device_ids=true | all-gather | bytes 640 | tf_op jit(solution)/shard_map/all_gather | solution.py:12
  28.0 13.3 %all-gather.1 = f32[32,4,1]{2,0,1:T(8,128)S(1)} all-gather(f32[8,4,1]{2,0,1:T(8,128)S(1)} %get-tuple-element.1667), channel_id=3, replica_groups=mesh['group'=2,'tm'=4,'tensor'=2,'dp'=2] {'tm'}, dimensions={0}, use_global_device_ids=true | all-gather | bytes 640 | tf_op jit(solution)/shard_map/all_gather | solution.py:12
  41.6 13.2 %all-gather.6 = f32[32,4,1]{2,0,1:T(8,128)S(1)} all-gather(f32[8,4,1]{2,0,1:T(8,128)S(1)} %neg.55), channel_id=8, replica_groups=mesh['group'=2,'tm'=4,'tensor'=2,'dp'=2] {'tm'}, dimensions={0}, use_global_device_ids=true | all-gather | bytes 640 | tf_op jit(solution)/shard_map/all_gather | solution.py:12
  79.1 145.3 %while.82 = (s32[]{:T(128)}, f32[8,4,128]{2,0,1:T(8,128)S(1)}, f32[8,4,128]{2,0,1:T(8,128)S(1)}, f32[6,128,4,128]{3,1,0,2:T(8,128)}, f32[6,8,4,128]{3,1,2,0:T(8,...) while((s32[]{:T(128)}, f32[8,4,128]{2,0,1:T(8,128)S(1)}, ...), condition=%wide.region_4.5_spmd.clone.clone, body=%wide.region_3.4_spmd.clone.clone.sunk | while | flops 1623294208 | bytes 7542485 | solution.py:124
  82.1 10.2 %multiply_reduce_fusion.11 = (f32[4,128,128]{1,2,0:T(8,128)S(1)}, f32[8,4,128,128]{3,2,0,1:T(8,128)S(1)}) fusion(f32[4,128,8]{1,2,0:T(8,128)S(1)} %copy.360, f32[8,4,128]{2,0,1:T(8,128)S(1)} %get-tuple-element.2158, f32[8,4,128]{2,0,1:T(8,128)S(1)} %bitcast.427, f32[8,4,128]{2,0,1:T(8,128)S(1)} %get-tuple-element.2159, ...), kind=kOutput, calls=%fused_computation.88.clone.1 | convolution fusion | flops 811532288 | bytes 2851584 | tf_op jit(solution)/shard_map/jvp()/while/body/eval_jaxpr/mhts,shd->mhtd/dot_general | solution.py:97
  92.3 10.3 %multiply_reduce_fusion.10 = (f32[4,128,128]{1,2,0:T(8,128)S(1)}, f32[8,4,128,128]{3,2,0,1:T(8,128)S(1)}) fusion(f32[4,128,8]{1,2,0:T(8,128)S(1)} %copy.359, f32[8,4,128]{2,0,1:T(8,128)S(1)} %get-tuple-element.2159, f32[8,4,128]{2,0,1:T(8,128)S(1)} %bitcast.428, f32[8,4,128]{2,0,1:T(8,128)S(1)} %get-tuple-element.2158, ...), kind=kOutput, calls=%fused_computation.89.clone.1 | convolution fusion | flops 811532288 | bytes 2851584 | tf_op jit(solution)/shard_map/jvp()/while/body/eval_jaxpr/mhts,shd->mhtd/dot_general | solution.py:94
  106.2 10.2 %multiply_reduce_fusion.11 = (f32[4,128,128]{1,2,0:T(8,128)S(1)}, f32[8,4,128,128]{3,2,0,1:T(8,128)S(1)}) fusion(f32[4,128,8]{1,2,0:T(8,128)S(1)} %copy.360, f32[8,4,128]{2,0,1:T(8,128)S(1)} %get-tuple-element.2158, f32[8,4,128]{2,0,1:T(8,128)S(1)} %bitcast.427, f32[8,4,128]{2,0,1:T(8,128)S(1)} %get-tuple-element.2159, ...), kind=kOutput, calls=%fused_computation.88.clone.1 | convolution fusion | flops 811532288 | bytes 2851584 | tf_op jit(solution)/shard_map/jvp()/while/body/eval_jaxpr/mhts,shd->mhtd/dot_general | solution.py:97
  116.4 10.3 %multiply_reduce_fusion.10 = (f32[4,128,128]{1,2,0:T(8,128)S(1)}, f32[8,4,128,128]{3,2,0,1:T(8,128)S(1)}) fusion(f32[4,128,8]{1,2,0:T(8,128)S(1)} %copy.359, f32[8,4,128]{2,0,1:T(8,128)S(1)} %get-tuple-element.2159, f32[8,4,128]{2,0,1:T(8,128)S(1)} %bitcast.428, f32[8,4,128]{2,0,1:T(8,128)S(1)} %get-tuple-element.2158, ...), kind=kOutput, calls=%fused_computation.89.clone.1 | convolution fusion | flops 811532288 | bytes 2851584 | tf_op jit(solution)/shard_map/jvp()/while/body/eval_jaxpr/mhts,shd->mhtd/dot_general | solution.py:94
  130.4 10.2 %multiply_reduce_fusion.11 = (f32[4,128,128]{1,2,0:T(8,128)S(1)}, f32[8,4,128,128]{3,2,0,1:T(8,128)S(1)}) fusion(f32[4,128,8]{1,2,0:T(8,128)S(1)} %copy.360, f32[8,4,128]{2,0,1:T(8,128)S(1)} %get-tuple-element.2158, f32[8,4,128]{2,0,1:T(8,128)S(1)} %bitcast.427, f32[8,4,128]{2,0,1:T(8,128)S(1)} %get-tuple-element.2159, ...), kind=kOutput, calls=%fused_computation.88.clone.1 | convolution fusion | flops 811532288 | bytes 2851584 | tf_op jit(solution)/shard_map/jvp()/while/body/eval_jaxpr/mhts,shd->mhtd/dot_general | solution.py:97
  140.6 10.3 %multiply_reduce_fusion.10 = (f32[4,128,128]{1,2,0:T(8,128)S(1)}, f32[8,4,128,128]{3,2,0,1:T(8,128)S(1)}) fusion(f32[4,128,8]{1,2,0:T(8,128)S(1)} %copy.359, f32[8,4,128]{2,0,1:T(8,128)S(1)} %get-tuple-element.2159, f32[8,4,128]{2,0,1:T(8,128)S(1)} %bitcast.428, f32[8,4,128]{2,0,1:T(8,128)S(1)} %get-tuple-element.2158, ...), kind=kOutput, calls=%fused_computation.89.clone.1 | convolution fusion | flops 811532288 | bytes 2851584 | tf_op jit(solution)/shard_map/jvp()/while/body/eval_jaxpr/mhts,shd->mhtd/dot_general | solution.py:94
  154.5 10.2 %multiply_reduce_fusion.11 = (f32[4,128,128]{1,2,0:T(8,128)S(1)}, f32[8,4,128,128]{3,2,0,1:T(8,128)S(1)}) fusion(f32[4,128,8]{1,2,0:T(8,128)S(1)} %copy.360, f32[8,4,128]{2,0,1:T(8,128)S(1)} %get-tuple-element.2158, f32[8,4,128]{2,0,1:T(8,128)S(1)} %bitcast.427, f32[8,4,128]{2,0,1:T(8,128)S(1)} %get-tuple-element.2159, ...), kind=kOutput, calls=%fused_computation.88.clone.1 | convolution fusion | flops 811532288 | bytes 2851584 | tf_op jit(solution)/shard_map/jvp()/while/body/eval_jaxpr/mhts,shd->mhtd/dot_general | solution.py:97
  164.7 10.3 %multiply_reduce_fusion.10 = (f32[4,128,128]{1,2,0:T(8,128)S(1)}, f32[8,4,128,128]{3,2,0,1:T(8,128)S(1)}) fusion(f32[4,128,8]{1,2,0:T(8,128)S(1)} %copy.359, f32[8,4,128]{2,0,1:T(8,128)S(1)} %get-tuple-element.2159, f32[8,4,128]{2,0,1:T(8,128)S(1)} %bitcast.428, f32[8,4,128]{2,0,1:T(8,128)S(1)} %get-tuple-element.2158, ...), kind=kOutput, calls=%fused_computation.89.clone.1 | convolution fusion | flops 811532288 | bytes 2851584 | tf_op jit(solution)/shard_map/jvp()/while/body/eval_jaxpr/mhts,shd->mhtd/dot_general | solution.py:94
  178.6 10.2 %multiply_reduce_fusion.11 = (f32[4,128,128]{1,2,0:T(8,128)S(1)}, f32[8,4,128,128]{3,2,0,1:T(8,128)S(1)}) fusion(f32[4,128,8]{1,2,0:T(8,128)S(1)} %copy.360, f32[8,4,128]{2,0,1:T(8,128)S(1)} %get-tuple-element.2158, f32[8,4,128]{2,0,1:T(8,128)S(1)} %bitcast.427, f32[8,4,128]{2,0,1:T(8,128)S(1)} %get-tuple-element.2159, ...), kind=kOutput, calls=%fused_computation.88.clone.1 | convolution fusion | flops 811532288 | bytes 2851584 | tf_op jit(solution)/shard_map/jvp()/while/body/eval_jaxpr/mhts,shd->mhtd/dot_general | solution.py:97
  188.8 10.3 %multiply_reduce_fusion.10 = (f32[4,128,128]{1,2,0:T(8,128)S(1)}, f32[8,4,128,128]{3,2,0,1:T(8,128)S(1)}) fusion(f32[4,128,8]{1,2,0:T(8,128)S(1)} %copy.359, f32[8,4,128]{2,0,1:T(8,128)S(1)} %get-tuple-element.2159, f32[8,4,128]{2,0,1:T(8,128)S(1)} %bitcast.428, f32[8,4,128]{2,0,1:T(8,128)S(1)} %get-tuple-element.2158, ...), kind=kOutput, calls=%fused_computation.89.clone.1 | convolution fusion | flops 811532288 | bytes 2851584 | tf_op jit(solution)/shard_map/jvp()/while/body/eval_jaxpr/mhts,shd->mhtd/dot_general | solution.py:94
  202.7 10.2 %multiply_reduce_fusion.11 = (f32[4,128,128]{1,2,0:T(8,128)S(1)}, f32[8,4,128,128]{3,2,0,1:T(8,128)S(1)}) fusion(f32[4,128,8]{1,2,0:T(8,128)S(1)} %copy.360, f32[8,4,128]{2,0,1:T(8,128)S(1)} %get-tuple-element.2158, f32[8,4,128]{2,0,1:T(8,128)S(1)} %bitcast.427, f32[8,4,128]{2,0,1:T(8,128)S(1)} %get-tuple-element.2159, ...), kind=kOutput, calls=%fused_computation.88.clone.1 | convolution fusion | flops 811532288 | bytes 2851584 | tf_op jit(solution)/shard_map/jvp()/while/body/eval_jaxpr/mhts,shd->mhtd/dot_general | solution.py:97
  212.9 10.3 %multiply_reduce_fusion.10 = (f32[4,128,128]{1,2,0:T(8,128)S(1)}, f32[8,4,128,128]{3,2,0,1:T(8,128)S(1)}) fusion(f32[4,128,8]{1,2,0:T(8,128)S(1)} %copy.359, f32[8,4,128]{2,0,1:T(8,128)S(1)} %get-tuple-element.2159, f32[8,4,128]{2,0,1:T(8,128)S(1)} %bitcast.428, f32[8,4,128]{2,0,1:T(8,128)S(1)} %get-tuple-element.2158, ...), kind=kOutput, calls=%fused_computation.89.clone.1 | convolution fusion | flops 811532288 | bytes 2851584 | tf_op jit(solution)/shard_map/jvp()/while/body/eval_jaxpr/mhts,shd->mhtd/dot_general | solution.py:94
  227.4 13.2 %all-gather.2 = f32[32,4,128]{2,0,1:T(8,128)S(1)} all-gather(f32[8,4,128]{2,0,1:T(8,128)S(1)} %get-tuple-element.821), channel_id=4, replica_groups=mesh['group'=2,'tm'=4,'tensor'=2,'dp'=2] {'tm'}, dimensions={0}, use_global_device_ids=true | all-gather | bytes 81920 | tf_op jit(solution)/shard_map/all_gather | solution.py:12
  240.6 13.2 %all-gather.3 = f32[32,4,128]{2,0,1:T(8,128)S(1)} all-gather(f32[8,4,128]{2,0,1:T(8,128)S(1)} %get-tuple-element.822), channel_id=5, replica_groups=mesh['group'=2,'tm'=4,'tensor'=2,'dp'=2] {'tm'}, dimensions={0}, use_global_device_ids=true | all-gather | bytes 81920 | tf_op jit(solution)/shard_map/all_gather | solution.py:12
  260.5 13.2 %all-gather.4 = f32[32,4,128]{2,0,1:T(8,128)S(1)} all-gather(f32[8,4,128]{2,0,1:T(8,128)S(1)} %get-tuple-element.1700), channel_id=6, replica_groups=mesh['group'=2,'tm'=4,'tensor'=2,'dp'=2] {'tm'}, dimensions={0}, use_global_device_ids=true | all-gather | bytes 81920 | tf_op jit(solution)/shard_map/all_gather | solution.py:12
  273.7 13.2 %all-gather.5 = f32[32,4,128]{2,0,1:T(8,128)S(1)} all-gather(f32[8,4,128]{2,0,1:T(8,128)S(1)} %get-tuple-element.1664), channel_id=7, replica_groups=mesh['group'=2,'tm'=4,'tensor'=2,'dp'=2] {'tm'}, dimensions={0}, use_global_device_ids=true | all-gather | bytes 81920 | tf_op jit(solution)/shard_map/all_gather | solution.py:12
  290.1 313.4 %while.83 = (s32[]{:T(128)}, f32[4,128]{1,0:T(4,128)S(1)}, f32[8,4,128]{2,1,0:T(4,128)}, f32[8,4,128]{2,1,0:T(4,128)}, f32[8,4,128]{2,0,1:T(8,128)}, /*index=5*/...) while((s32[]{:T(128)}, f32[4,128]{1,0:T(4,128)S(1)}, ...), condition=%wide.region_15.16_spmd.clone.clone.clone, body=%wide.region_9.15_spmd.clone.clone.clone.sunk | while | flops 3254166272 | bytes 45512152 | solution.py:124
  290.3 10.1 %fusion.192 = (f32[8,4,128,128]{3,2,0,1:T(8,128)}, f32[8,4,128,128]{3,2,0,1:T(8,128)}) fusion(f32[8,4]{0,1:T(4,128)S(1)} %get-tuple-element.2326, f32[128,128]{1,0:T(8,128)} %get-tuple-element.2325, f32[8,4]{0,1:T(4,128)S(1)} %get-tuple-element.2323, pred[128,128]{1,0:T(8,128)(4,1)S(1)} %get-tuple-element.2324), kind=kLoop, calls=%fused_computation.23.clone.1 | loop fusion | flops 2621440 | bytes 4276480 | tf_op jit(solution)/shard_map/mul | solution.py:57
  320.0 4.5 fusion.195
  328.7 6.1 multiply_reduce_fusion.12
  342.5 10.1 %fusion.192 = (f32[8,4,128,128]{3,2,0,1:T(8,128)}, f32[8,4,128,128]{3,2,0,1:T(8,128)}) fusion(f32[8,4]{0,1:T(4,128)S(1)} %get-tuple-element.2326, f32[128,128]{1,0:T(8,128)} %get-tuple-element.2325, f32[8,4]{0,1:T(4,128)S(1)} %get-tuple-element.2323, pred[128,128]{1,0:T(8,128)(4,1)S(1)} %get-tuple-element.2324), kind=kLoop, calls=%fused_computation.23.clone.1 | loop fusion | flops 2621440 | bytes 4276480 | tf_op jit(solution)/shard_map/mul | solution.py:57
  363.3 4.5 fusion.194
  372.1 4.5 fusion.195
  380.9 6.1 multiply_reduce_fusion.12
  394.7 10.1 %fusion.192 = (f32[8,4,128,128]{3,2,0,1:T(8,128)}, f32[8,4,128,128]{3,2,0,1:T(8,128)}) fusion(f32[8,4]{0,1:T(4,128)S(1)} %get-tuple-element.2326, f32[128,128]{1,0:T(8,128)} %get-tuple-element.2325, f32[8,4]{0,1:T(4,128)S(1)} %get-tuple-element.2323, pred[128,128]{1,0:T(8,128)(4,1)S(1)} %get-tuple-element.2324), kind=kLoop, calls=%fused_computation.23.clone.1 | loop fusion | flops 2621440 | bytes 4276480 | tf_op jit(solution)/shard_map/mul | solution.py:57
  424.3 4.5 fusion.195
  433.1 6.1 multiply_reduce_fusion.12
  446.9 10.1 %fusion.192 = (f32[8,4,128,128]{3,2,0,1:T(8,128)}, f32[8,4,128,128]{3,2,0,1:T(8,128)}) fusion(f32[8,4]{0,1:T(4,128)S(1)} %get-tuple-element.2326, f32[128,128]{1,0:T(8,128)} %get-tuple-element.2325, f32[8,4]{0,1:T(4,128)S(1)} %get-tuple-element.2323, pred[128,128]{1,0:T(8,128)(4,1)S(1)} %get-tuple-element.2324), kind=kLoop, calls=%fused_computation.23.clone.1 | loop fusion | flops 2621440 | bytes 4276480 | tf_op jit(solution)/shard_map/mul | solution.py:57
  467.6 4.5 fusion.194
  476.5 4.5 fusion.195
  485.3 6.1 multiply_reduce_fusion.12
  499.1 10.1 %fusion.192 = (f32[8,4,128,128]{3,2,0,1:T(8,128)}, f32[8,4,128,128]{3,2,0,1:T(8,128)}) fusion(f32[8,4]{0,1:T(4,128)S(1)} %get-tuple-element.2326, f32[128,128]{1,0:T(8,128)} %get-tuple-element.2325, f32[8,4]{0,1:T(4,128)S(1)} %get-tuple-element.2323, pred[128,128]{1,0:T(8,128)(4,1)S(1)} %get-tuple-element.2324), kind=kLoop, calls=%fused_computation.23.clone.1 | loop fusion | flops 2621440 | bytes 4276480 | tf_op jit(solution)/shard_map/mul | solution.py:57
  519.8 4.5 fusion.194
  528.7 4.5 fusion.195
  537.4 6.1 multiply_reduce_fusion.12
  551.3 10.1 %fusion.192 = (f32[8,4,128,128]{3,2,0,1:T(8,128)}, f32[8,4,128,128]{3,2,0,1:T(8,128)}) fusion(f32[8,4]{0,1:T(4,128)S(1)} %get-tuple-element.2326, f32[128,128]{1,0:T(8,128)} %get-tuple-element.2325, f32[8,4]{0,1:T(4,128)S(1)} %get-tuple-element.2323, pred[128,128]{1,0:T(8,128)(4,1)S(1)} %get-tuple-element.2324), kind=kLoop, calls=%fused_computation.23.clone.1 | loop fusion | flops 2621440 | bytes 4276480 | tf_op jit(solution)/shard_map/mul | solution.py:57
  580.9 4.5 fusion.195
  589.6 6.1 multiply_reduce_fusion.12
  607.7 5.7 multiply_bitcast_fusion
  614.5 4.7 convolution_bitcast_fusion
  621.7 29.1 %all-reduce.6 = (f32[2,8,512]{2,1,0:T(8,128)}, f32[512]{0:T(512)}) all-reduce(f32[2,8,512]{2,1,0:T(8,128)S(1)} %add_multiply_fusion, f32[512]{0:T(512)S(1)} %multiply_bitcast_fusion.3), channel_id=1, replica_groups=mesh['group'=2,'tm'=4,'tensor'=2,'dp'=2] {'tm','dp'}, use_global_device_ids=true, to_apply=%region_18.19 | all-reduce | flops 8704 | bytes 69632 | tf_op jit(solution)/shard_map/psum | solution.py:183
  650.8 61.4 %all-reduce.9.cloned.1.call-done = f32[2,1024,512]{1,2,0:T(8,128)} async-done(((f32[2,1024,512]{1,2,0:T(8,128)}), f32[2,1024,512]{1,2,0:T(8,128)}) %all-reduce.9.cloned.1.call-update) | async-done | bytes 4194320 | tf_op jit(solution)/shard_map/psum | solution.py:183
  712.2 5.4 copy.231
  717.5 40.3 %reduce-scatter.2.cloned.1.call-done = f32[1,768,512]{2,1,0:T(8,128)} async-done(((f32[1,768,1024]{2,1,0:T(8,128)}), f32[1,768,512]{2,1,0:T(8,128)}) %reduce-scatter.2.cloned.1.call-update) | async-done | bytes 1572880 | tf_op jit(solution)/shard_map/reduce_scatter | solution.py:173
  (663 shorter events, 248.8 us)
Async XLA Ops:
  7.2 48.8 %copy-start = (bf16[2,1024,512]{2,1,0:T(8,128)(2,1)S(1)}, bf16[2,1024,512]{2,1,0:T(8,128)(2,1)}, u32[]{:S(2)}) copy-start(bf16[2,1024,512]{2,1,0:T(8,128)(2,1)} %param.17) | copy-start | bytes 6291460
  7.2 48.7 %all-gather.9.cloned.1.call-start = ((), (), s32[]{:S(2)}) async-start(), calls=%async_computation.1 | async-start | bytes 2359296 | tf_op jit(solution)/shard_map/all_gather | solution.py:45
  7.9 704.2 %all-reduce.9.cloned.1.call-start = ((), (), s32[]{:S(2)}) async-start(), calls=%async_computation.3 | async-start | bytes 8388608 | tf_op jit(solution)/shard_map/psum | solution.py:183
  11.7 248.1 %copy-start.38 = (f32[8,4]{0,1:T(4,128)}, f32[8,4]{0,1:T(4,128)S(1)}, u32[]{:S(2)}) copy-start(f32[8,4]{0,1:T(4,128)S(1)} %get-tuple-element.1705) | copy-start | bytes 388
  259.8 30.4 %copy-start.31 = (f32[4,128]{1,0:T(4,128)S(1)}, f32[4,128]{1,0:T(4,128)}, u32[]{:S(2)}) copy-start(f32[4,128]{1,0:T(4,128)} %custom-call.4) | copy-start | bytes 6148
  290.3 10.2 %copy-start.11 = (pred[128,128]{1,0:T(8,128)(4,1)}, pred[128,128]{1,0:T(8,128)(4,1)S(1)}, u32[]{:S(2)}) copy-start(pred[128,128]{1,0:T(8,128)(4,1)S(1)} %get-tuple-element.2324) | copy-start | bytes 49156 | tf_op jit(solution)/shard_map/transpose(jvp())/while
  290.3 10.1 %copy-start.21 = (f32[8,4]{0,1:T(4,128)}, f32[8,4]{0,1:T(4,128)S(1)}, u32[]{:S(2)}) copy-start(f32[8,4]{0,1:T(4,128)S(1)} %get-tuple-element.2323) | copy-start | bytes 388 | tf_op jit(solution)/shard_map/transpose(jvp())/while
  290.3 10.1 %copy-start.24 = (f32[8,4]{0,1:T(4,128)}, f32[8,4]{0,1:T(4,128)S(1)}, u32[]{:S(2)}) copy-start(f32[8,4]{0,1:T(4,128)S(1)} %get-tuple-element.2326) | copy-start | bytes 388 | tf_op jit(solution)/shard_map/transpose(jvp())/while
  290.3 10.1 %copy-start.27 = (f32[4,128]{1,0:T(4,128)}, f32[4,128]{1,0:T(4,128)S(1)}, u32[]{:S(2)}) copy-start(f32[4,128]{1,0:T(4,128)S(1)} %get-tuple-element.2137) | copy-start | bytes 6148 | tf_op jit(solution)/shard_map/transpose(jvp())/while
  290.3 12.7 %copy-start.40 = (s32[6,128]{1,0:T(8,128)}, s32[6,128]{1,0:T(8,128)S(1)}, u32[]{:S(2)}) copy-start(s32[6,128]{1,0:T(8,128)S(1)} %get-tuple-element.2315) | copy-start | bytes 9220 | tf_op jit(solution)/shard_map/transpose(jvp())/while
  290.3 12.7 %copy-start.45 = (s32[6]{0:T(128)}, s32[6]{0:T(128)S(1)}, u32[]{:S(2)}) copy-start(s32[6]{0:T(128)S(1)} %get-tuple-element.2316) | copy-start | bytes 76 | tf_op jit(solution)/shard_map/transpose(jvp())/while
  328.7 7.3 copy-start.1
  342.5 10.2 %copy-start.11 = (pred[128,128]{1,0:T(8,128)(4,1)}, pred[128,128]{1,0:T(8,128)(4,1)S(1)}, u32[]{:S(2)}) copy-start(pred[128,128]{1,0:T(8,128)(4,1)S(1)} %get-tuple-element.2324) | copy-start | bytes 49156 | tf_op jit(solution)/shard_map/transpose(jvp())/while
  342.5 10.1 %copy-start.21 = (f32[8,4]{0,1:T(4,128)}, f32[8,4]{0,1:T(4,128)S(1)}, u32[]{:S(2)}) copy-start(f32[8,4]{0,1:T(4,128)S(1)} %get-tuple-element.2323) | copy-start | bytes 388 | tf_op jit(solution)/shard_map/transpose(jvp())/while
  342.5 10.1 %copy-start.24 = (f32[8,4]{0,1:T(4,128)}, f32[8,4]{0,1:T(4,128)S(1)}, u32[]{:S(2)}) copy-start(f32[8,4]{0,1:T(4,128)S(1)} %get-tuple-element.2326) | copy-start | bytes 388 | tf_op jit(solution)/shard_map/transpose(jvp())/while
  342.5 10.1 %copy-start.27 = (f32[4,128]{1,0:T(4,128)}, f32[4,128]{1,0:T(4,128)S(1)}, u32[]{:S(2)}) copy-start(f32[4,128]{1,0:T(4,128)S(1)} %get-tuple-element.2137) | copy-start | bytes 6148 | tf_op jit(solution)/shard_map/transpose(jvp())/while
  342.5 12.7 %copy-start.40 = (s32[6,128]{1,0:T(8,128)}, s32[6,128]{1,0:T(8,128)S(1)}, u32[]{:S(2)}) copy-start(s32[6,128]{1,0:T(8,128)S(1)} %get-tuple-element.2315) | copy-start | bytes 9220 | tf_op jit(solution)/shard_map/transpose(jvp())/while
  342.5 12.7 %copy-start.45 = (s32[6]{0:T(128)}, s32[6]{0:T(128)S(1)}, u32[]{:S(2)}) copy-start(s32[6]{0:T(128)S(1)} %get-tuple-element.2316) | copy-start | bytes 76 | tf_op jit(solution)/shard_map/transpose(jvp())/while
  380.9 7.3 copy-start.1
  394.7 10.2 %copy-start.11 = (pred[128,128]{1,0:T(8,128)(4,1)}, pred[128,128]{1,0:T(8,128)(4,1)S(1)}, u32[]{:S(2)}) copy-start(pred[128,128]{1,0:T(8,128)(4,1)S(1)} %get-tuple-element.2324) | copy-start | bytes 49156 | tf_op jit(solution)/shard_map/transpose(jvp())/while
  394.7 10.1 %copy-start.21 = (f32[8,4]{0,1:T(4,128)}, f32[8,4]{0,1:T(4,128)S(1)}, u32[]{:S(2)}) copy-start(f32[8,4]{0,1:T(4,128)S(1)} %get-tuple-element.2323) | copy-start | bytes 388 | tf_op jit(solution)/shard_map/transpose(jvp())/while
  394.7 10.1 %copy-start.24 = (f32[8,4]{0,1:T(4,128)}, f32[8,4]{0,1:T(4,128)S(1)}, u32[]{:S(2)}) copy-start(f32[8,4]{0,1:T(4,128)S(1)} %get-tuple-element.2326) | copy-start | bytes 388 | tf_op jit(solution)/shard_map/transpose(jvp())/while
  394.7 10.1 %copy-start.27 = (f32[4,128]{1,0:T(4,128)}, f32[4,128]{1,0:T(4,128)S(1)}, u32[]{:S(2)}) copy-start(f32[4,128]{1,0:T(4,128)S(1)} %get-tuple-element.2137) | copy-start | bytes 6148 | tf_op jit(solution)/shard_map/transpose(jvp())/while
  394.7 12.7 %copy-start.40 = (s32[6,128]{1,0:T(8,128)}, s32[6,128]{1,0:T(8,128)S(1)}, u32[]{:S(2)}) copy-start(s32[6,128]{1,0:T(8,128)S(1)} %get-tuple-element.2315) | copy-start | bytes 9220 | tf_op jit(solution)/shard_map/transpose(jvp())/while
  394.7 12.7 %copy-start.45 = (s32[6]{0:T(128)}, s32[6]{0:T(128)S(1)}, u32[]{:S(2)}) copy-start(s32[6]{0:T(128)S(1)} %get-tuple-element.2316) | copy-start | bytes 76 | tf_op jit(solution)/shard_map/transpose(jvp())/while
  433.1 7.3 copy-start.1
  446.8 10.2 %copy-start.11 = (pred[128,128]{1,0:T(8,128)(4,1)}, pred[128,128]{1,0:T(8,128)(4,1)S(1)}, u32[]{:S(2)}) copy-start(pred[128,128]{1,0:T(8,128)(4,1)S(1)} %get-tuple-element.2324) | copy-start | bytes 49156 | tf_op jit(solution)/shard_map/transpose(jvp())/while
  446.8 10.1 %copy-start.21 = (f32[8,4]{0,1:T(4,128)}, f32[8,4]{0,1:T(4,128)S(1)}, u32[]{:S(2)}) copy-start(f32[8,4]{0,1:T(4,128)S(1)} %get-tuple-element.2323) | copy-start | bytes 388 | tf_op jit(solution)/shard_map/transpose(jvp())/while
  446.9 10.1 %copy-start.24 = (f32[8,4]{0,1:T(4,128)}, f32[8,4]{0,1:T(4,128)S(1)}, u32[]{:S(2)}) copy-start(f32[8,4]{0,1:T(4,128)S(1)} %get-tuple-element.2326) | copy-start | bytes 388 | tf_op jit(solution)/shard_map/transpose(jvp())/while
  446.9 10.1 %copy-start.27 = (f32[4,128]{1,0:T(4,128)}, f32[4,128]{1,0:T(4,128)S(1)}, u32[]{:S(2)}) copy-start(f32[4,128]{1,0:T(4,128)S(1)} %get-tuple-element.2137) | copy-start | bytes 6148 | tf_op jit(solution)/shard_map/transpose(jvp())/while
  446.9 12.7 %copy-start.40 = (s32[6,128]{1,0:T(8,128)}, s32[6,128]{1,0:T(8,128)S(1)}, u32[]{:S(2)}) copy-start(s32[6,128]{1,0:T(8,128)S(1)} %get-tuple-element.2315) | copy-start | bytes 9220 | tf_op jit(solution)/shard_map/transpose(jvp())/while
  446.9 12.7 %copy-start.45 = (s32[6]{0:T(128)}, s32[6]{0:T(128)S(1)}, u32[]{:S(2)}) copy-start(s32[6]{0:T(128)S(1)} %get-tuple-element.2316) | copy-start | bytes 76 | tf_op jit(solution)/shard_map/transpose(jvp())/while
  485.2 7.3 copy-start.1
  499.0 10.2 %copy-start.11 = (pred[128,128]{1,0:T(8,128)(4,1)}, pred[128,128]{1,0:T(8,128)(4,1)S(1)}, u32[]{:S(2)}) copy-start(pred[128,128]{1,0:T(8,128)(4,1)S(1)} %get-tuple-element.2324) | copy-start | bytes 49156 | tf_op jit(solution)/shard_map/transpose(jvp())/while
  499.0 10.1 %copy-start.21 = (f32[8,4]{0,1:T(4,128)}, f32[8,4]{0,1:T(4,128)S(1)}, u32[]{:S(2)}) copy-start(f32[8,4]{0,1:T(4,128)S(1)} %get-tuple-element.2323) | copy-start | bytes 388 | tf_op jit(solution)/shard_map/transpose(jvp())/while
  499.0 10.1 %copy-start.24 = (f32[8,4]{0,1:T(4,128)}, f32[8,4]{0,1:T(4,128)S(1)}, u32[]{:S(2)}) copy-start(f32[8,4]{0,1:T(4,128)S(1)} %get-tuple-element.2326) | copy-start | bytes 388 | tf_op jit(solution)/shard_map/transpose(jvp())/while
  499.0 10.1 %copy-start.27 = (f32[4,128]{1,0:T(4,128)}, f32[4,128]{1,0:T(4,128)S(1)}, u32[]{:S(2)}) copy-start(f32[4,128]{1,0:T(4,128)S(1)} %get-tuple-element.2137) | copy-start | bytes 6148 | tf_op jit(solution)/shard_map/transpose(jvp())/while
  499.1 12.7 %copy-start.40 = (s32[6,128]{1,0:T(8,128)}, s32[6,128]{1,0:T(8,128)S(1)}, u32[]{:S(2)}) copy-start(s32[6,128]{1,0:T(8,128)S(1)} %get-tuple-element.2315) | copy-start | bytes 9220 | tf_op jit(solution)/shard_map/transpose(jvp())/while
  499.1 12.7 %copy-start.45 = (s32[6]{0:T(128)}, s32[6]{0:T(128)S(1)}, u32[]{:S(2)}) copy-start(s32[6]{0:T(128)S(1)} %get-tuple-element.2316) | copy-start | bytes 76 | tf_op jit(solution)/shard_map/transpose(jvp())/while
  537.4 7.3 copy-start.1
  551.2 10.2 %copy-start.11 = (pred[128,128]{1,0:T(8,128)(4,1)}, pred[128,128]{1,0:T(8,128)(4,1)S(1)}, u32[]{:S(2)}) copy-start(pred[128,128]{1,0:T(8,128)(4,1)S(1)} %get-tuple-element.2324) | copy-start | bytes 49156 | tf_op jit(solution)/shard_map/transpose(jvp())/while
  551.2 10.1 %copy-start.21 = (f32[8,4]{0,1:T(4,128)}, f32[8,4]{0,1:T(4,128)S(1)}, u32[]{:S(2)}) copy-start(f32[8,4]{0,1:T(4,128)S(1)} %get-tuple-element.2323) | copy-start | bytes 388 | tf_op jit(solution)/shard_map/transpose(jvp())/while
  551.2 10.1 %copy-start.24 = (f32[8,4]{0,1:T(4,128)}, f32[8,4]{0,1:T(4,128)S(1)}, u32[]{:S(2)}) copy-start(f32[8,4]{0,1:T(4,128)S(1)} %get-tuple-element.2326) | copy-start | bytes 388 | tf_op jit(solution)/shard_map/transpose(jvp())/while
  551.2 10.1 %copy-start.27 = (f32[4,128]{1,0:T(4,128)}, f32[4,128]{1,0:T(4,128)S(1)}, u32[]{:S(2)}) copy-start(f32[4,128]{1,0:T(4,128)S(1)} %get-tuple-element.2137) | copy-start | bytes 6148 | tf_op jit(solution)/shard_map/transpose(jvp())/while
  551.2 12.7 %copy-start.40 = (s32[6,128]{1,0:T(8,128)}, s32[6,128]{1,0:T(8,128)S(1)}, u32[]{:S(2)}) copy-start(s32[6,128]{1,0:T(8,128)S(1)} %get-tuple-element.2315) | copy-start | bytes 9220 | tf_op jit(solution)/shard_map/transpose(jvp())/while
  551.2 12.7 %copy-start.45 = (s32[6]{0:T(128)}, s32[6]{0:T(128)S(1)}, u32[]{:S(2)}) copy-start(s32[6]{0:T(128)S(1)} %get-tuple-element.2316) | copy-start | bytes 76 | tf_op jit(solution)/shard_map/transpose(jvp())/while
  589.6 7.3 copy-start.1
  613.4 144.4 %reduce-scatter.2.cloned.1.call-start = ((), (), s32[]{:S(2)}) async-start(), calls=%async_computation.2 | async-start | bytes 4718592 | tf_op jit(solution)/shard_map/reduce_scatter | solution.py:173
  (137 other events, 530.1 us)
Sparse Core Ops, SparseCore 0:
  9.6 29.8 all-gather.8
  613.5 98.6 all-reduce.8
  714.4 43.3 reduce-scatter.1
where the time goes:
time: 777 us; the launch traced here: 767 us
  matrix products  288 us (37%)
  other arithmetic  130 us (17%)
  blocking collectives  123 us (16%)
  local copies, waits for them, and re-layouts  104 us (13%)
  waiting for transfers between devices  102 us (13%)
  between operations  15.1 us (2%)
    dot_general x18, matrix products, block_step(): jnp.einsum('mhts,shd->mhtd', kern_re * same_clip, block_in, precision=lar...  108 us
    dot_general x18, matrix products, block_step(): jnp.einsum('mhts,shd->mhtd', kern_im * same_clip, block_in, precision=lar...  102 us
    all_gather x7, blocking collectives, carried_in(): pieces = jax.tree.map(lambda part: lax.all_gather(part, axis), value)  94.2 us
    psum x1, waiting for transfers between devices, shards(): lax.psum((proj_term, coeff_term, skip_term), ('tm', 'dp'))  61.4 us
    mul x6, other arithmetic, shards(): kern_im = damping * jnp.sin(angles[:, :, None, None] * lag_steps)  60.6 us
    reduce_scatter x1, waiting for transfers between devices, shards(): lax.psum_scatter(partial_in[None], 'tensor', scatter_dimension=2, tiled=T...  40.3 us
    reduce_sum x6, other arithmetic, block_step(): block_re[..., None] * state_im[:, :, None, :]  36.6 us
    dynamic_slice x36, local copies, waits for them, and re-layouts, intra(): lax.scan(jax.checkpoint(block_step), (initial, initial), (blocks_in, seg_...  30.9 us
  transfers between devices with their start and end apart: 3, of which 2 were waited for; matrix products, arithmetic and copies ran while one was open for 2% of the time, Pallas kernels for 0%

commit v1 on v0

--- a/solution.py
+++ b/solution.py
@@ -180,7 +180,9 @@
     )
     coeff_term = (coeff_local + coeff_carry) * norm_scale
     skip_term = skip_local * norm_scale
-    proj_sum, coeff_sum, skip_sum = lax.psum((proj_term, coeff_term, skip_term), ("tm", "dp"))
+    proj_sum, coeff_sum, skip_sum = lax.psum(
+        lax.psum((proj_term, coeff_term, skip_term), "dp"), "tm"
+    )
     return (mixed[None], input_grad, proj_sum, coeff_sum, skip_sum)
 
 

time: 777 us -> 869 us (1.12)
  waiting for transfers between devices: 102 us -> 200 us
    psum x1 -> x2, waiting for transfers between devices: 61.4 us -> 178 us  [the longest x1 155 us: shards(): lax.psum(lax.psum((proj_term, coeff_term, skip_term), 'dp'), 'tm')]
    reduce_scatter x1, waiting for transfers between devices: 40.3 us -> 20.7 us  [shards(): lax.psum_scatter(partial_in[None], 'tensor', scatter_dimension=2, tiled=T...]
    psum x1 -> x2, blocking collectives: 29.1 us -> 23.8 us  [the longest x1 20.3 us: shards(): lax.psum(lax.psum((proj_term, coeff_term, skip_term), 'dp'), 'tm')]
  transfers between devices with their start and end apart: 3 -> 4, of which waited for: 2 -> 3; matrix products, arithmetic and copies ran while one was open for 2% -> 2% of each run, Pallas kernels for 0% -> 0%
where the time goes in v1:
time: 869 us; the launch traced here: 859 us
  matrix products  288 us (33%)
  waiting for transfers between devices  200 us (23%)
  other arithmetic  131 us (15%)
  blocking collectives  118 us (14%)
  local copies, waits for them, and re-layouts  103 us (12%)
  between operations  15.1 us (2%)
    psum x1, waiting for transfers between devices, shards(): lax.psum(lax.psum((proj_term, coeff_term, skip_term), 'dp'), 'tm')  155 us
    dot_general x18, matrix products, block_step(): jnp.einsum('mhts,shd->mhtd', kern_re * same_clip, block_in, precision=lar...  108 us
    dot_general x18, matrix products, block_step(): jnp.einsum('mhts,shd->mhtd', kern_im * same_clip, block_in, precision=lar...  102 us
    all_gather x7, blocking collectives, carried_in(): pieces = jax.tree.map(lambda part: lax.all_gather(part, axis), value)  94.2 us
    mul x6, other arithmetic, shards(): kern_im = damping * jnp.sin(angles[:, :, None, None] * lag_steps)  60.5 us
    reduce_sum x6, other arithmetic, block_step(): block_re[..., None] * state_im[:, :, None, :]  36.6 us
    dynamic_slice x36, local copies, waits for them, and re-layouts, intra(): lax.scan(jax.checkpoint(block_step), (initial, initial), (blocks_in, seg_...  30.8 us
    dot_general x6, matrix products, block_step(): jnp.einsum('ywo,ywlo->lwo', coefficient_imaginary, aggregate_imaginary, p...  27 us
  transfers between devices with their start and end apart: 4, of which 3 were waited for; matrix products, arithmetic and copies ran while one was open for 2% of the time, Pallas kernels for 0%

profile of v1, /device:TPU:0, one launch (start us, length us, event | category | flops | bytes accessed | tf_op | source)
XLA Modules:
  0.0 858.9 jit_solution(495196602819910565)
XLA Ops:
  13.1 14.9 %all-gather = f32[32,4,1]{2,0,1:T(8,128)S(1)} all-gather(f32[8,4,1]{2,0,1:T(8,128)S(1)} %get-tuple-element.1670), channel_id=2, replica_groups=mesh['group'=2,'tm'=4,'tensor'=2,'dp'=2] {'tm'}, dimensions={0}, use_global_device_ids=true | all-gather | bytes 640 | tf_op jit(solution)/shard_map/all_gather | solution.py:12
  28.2 13.3 %all-gather.1 = f32[32,4,1]{2,0,1:T(8,128)S(1)} all-gather(f32[8,4,1]{2,0,1:T(8,128)S(1)} %get-tuple-element.1669), channel_id=3, replica_groups=mesh['group'=2,'tm'=4,'tensor'=2,'dp'=2] {'tm'}, dimensions={0}, use_global_device_ids=true | all-gather | bytes 640 | tf_op jit(solution)/shard_map/all_gather | solution.py:12
  41.7 13.2 %all-gather.6 = f32[32,4,1]{2,0,1:T(8,128)S(1)} all-gather(f32[8,4,1]{2,0,1:T(8,128)S(1)} %neg.55), channel_id=8, replica_groups=mesh['group'=2,'tm'=4,'tensor'=2,'dp'=2] {'tm'}, dimensions={0}, use_global_device_ids=true | all-gather | bytes 640 | tf_op jit(solution)/shard_map/all_gather | solution.py:12
  79.2 146.0 %while.82 = (s32[]{:T(128)}, f32[8,4,128]{2,0,1:T(8,128)S(1)}, f32[8,4,128]{2,0,1:T(8,128)S(1)}, f32[6,128,4,128]{3,1,0,2:T(8,128)}, f32[6,8,4,128]{3,1,2,0:T(8,...) while((s32[]{:T(128)}, f32[8,4,128]{2,0,1:T(8,128)S(1)}, ...), condition=%wide.region_4.5_spmd.clone.clone, body=%wide.region_3.4_spmd.clone.clone.sunk | while | flops 1623294208 | bytes 7542485 | solution.py:124
  82.3 10.2 %multiply_reduce_fusion.11 = (f32[4,128,128]{1,2,0:T(8,128)S(1)}, f32[8,4,128,128]{3,2,0,1:T(8,128)S(1)}) fusion(f32[4,128,8]{1,2,0:T(8,128)S(1)} %copy.360, f32[8,4,128]{2,0,1:T(8,128)S(1)} %get-tuple-element.2160, f32[8,4,128]{2,0,1:T(8,128)S(1)} %bitcast.427, f32[8,4,128]{2,0,1:T(8,128)S(1)} %get-tuple-element.2161, ...), kind=kOutput, calls=%fused_computation.88.clone.1 | convolution fusion | flops 811532288 | bytes 2851584 | tf_op jit(solution)/shard_map/jvp()/while/body/eval_jaxpr/mhts,shd->mhtd/dot_general | solution.py:97
  92.5 10.3 %multiply_reduce_fusion.10 = (f32[4,128,128]{1,2,0:T(8,128)S(1)}, f32[8,4,128,128]{3,2,0,1:T(8,128)S(1)}) fusion(f32[4,128,8]{1,2,0:T(8,128)S(1)} %copy.359, f32[8,4,128]{2,0,1:T(8,128)S(1)} %get-tuple-element.2161, f32[8,4,128]{2,0,1:T(8,128)S(1)} %bitcast.428, f32[8,4,128]{2,0,1:T(8,128)S(1)} %get-tuple-element.2160, ...), kind=kOutput, calls=%fused_computation.89.clone.1 | convolution fusion | flops 811532288 | bytes 2851584 | tf_op jit(solution)/shard_map/jvp()/while/body/eval_jaxpr/mhts,shd->mhtd/dot_general | solution.py:94
  106.6 10.2 %multiply_reduce_fusion.11 = (f32[4,128,128]{1,2,0:T(8,128)S(1)}, f32[8,4,128,128]{3,2,0,1:T(8,128)S(1)}) fusion(f32[4,128,8]{1,2,0:T(8,128)S(1)} %copy.360, f32[8,4,128]{2,0,1:T(8,128)S(1)} %get-tuple-element.2160, f32[8,4,128]{2,0,1:T(8,128)S(1)} %bitcast.427, f32[8,4,128]{2,0,1:T(8,128)S(1)} %get-tuple-element.2161, ...), kind=kOutput, calls=%fused_computation.88.clone.1 | convolution fusion | flops 811532288 | bytes 2851584 | tf_op jit(solution)/shard_map/jvp()/while/body/eval_jaxpr/mhts,shd->mhtd/dot_general | solution.py:97
  116.8 10.3 %multiply_reduce_fusion.10 = (f32[4,128,128]{1,2,0:T(8,128)S(1)}, f32[8,4,128,128]{3,2,0,1:T(8,128)S(1)}) fusion(f32[4,128,8]{1,2,0:T(8,128)S(1)} %copy.359, f32[8,4,128]{2,0,1:T(8,128)S(1)} %get-tuple-element.2161, f32[8,4,128]{2,0,1:T(8,128)S(1)} %bitcast.428, f32[8,4,128]{2,0,1:T(8,128)S(1)} %get-tuple-element.2160, ...), kind=kOutput, calls=%fused_computation.89.clone.1 | convolution fusion | flops 811532288 | bytes 2851584 | tf_op jit(solution)/shard_map/jvp()/while/body/eval_jaxpr/mhts,shd->mhtd/dot_general | solution.py:94
  130.8 10.2 %multiply_reduce_fusion.11 = (f32[4,128,128]{1,2,0:T(8,128)S(1)}, f32[8,4,128,128]{3,2,0,1:T(8,128)S(1)}) fusion(f32[4,128,8]{1,2,0:T(8,128)S(1)} %copy.360, f32[8,4,128]{2,0,1:T(8,128)S(1)} %get-tuple-element.2160, f32[8,4,128]{2,0,1:T(8,128)S(1)} %bitcast.427, f32[8,4,128]{2,0,1:T(8,128)S(1)} %get-tuple-element.2161, ...), kind=kOutput, calls=%fused_computation.88.clone.1 | convolution fusion | flops 811532288 | bytes 2851584 | tf_op jit(solution)/shard_map/jvp()/while/body/eval_jaxpr/mhts,shd->mhtd/dot_general | solution.py:97
  141.0 10.3 %multiply_reduce_fusion.10 = (f32[4,128,128]{1,2,0:T(8,128)S(1)}, f32[8,4,128,128]{3,2,0,1:T(8,128)S(1)}) fusion(f32[4,128,8]{1,2,0:T(8,128)S(1)} %copy.359, f32[8,4,128]{2,0,1:T(8,128)S(1)} %get-tuple-element.2161, f32[8,4,128]{2,0,1:T(8,128)S(1)} %bitcast.428, f32[8,4,128]{2,0,1:T(8,128)S(1)} %get-tuple-element.2160, ...), kind=kOutput, calls=%fused_computation.89.clone.1 | convolution fusion | flops 811532288 | bytes 2851584 | tf_op jit(solution)/shard_map/jvp()/while/body/eval_jaxpr/mhts,shd->mhtd/dot_general | solution.py:94
  155.0 10.2 %multiply_reduce_fusion.11 = (f32[4,128,128]{1,2,0:T(8,128)S(1)}, f32[8,4,128,128]{3,2,0,1:T(8,128)S(1)}) fusion(f32[4,128,8]{1,2,0:T(8,128)S(1)} %copy.360, f32[8,4,128]{2,0,1:T(8,128)S(1)} %get-tuple-element.2160, f32[8,4,128]{2,0,1:T(8,128)S(1)} %bitcast.427, f32[8,4,128]{2,0,1:T(8,128)S(1)} %get-tuple-element.2161, ...), kind=kOutput, calls=%fused_computation.88.clone.1 | convolution fusion | flops 811532288 | bytes 2851584 | tf_op jit(solution)/shard_map/jvp()/while/body/eval_jaxpr/mhts,shd->mhtd/dot_general | solution.py:97
  165.2 10.3 %multiply_reduce_fusion.10 = (f32[4,128,128]{1,2,0:T(8,128)S(1)}, f32[8,4,128,128]{3,2,0,1:T(8,128)S(1)}) fusion(f32[4,128,8]{1,2,0:T(8,128)S(1)} %copy.359, f32[8,4,128]{2,0,1:T(8,128)S(1)} %get-tuple-element.2161, f32[8,4,128]{2,0,1:T(8,128)S(1)} %bitcast.428, f32[8,4,128]{2,0,1:T(8,128)S(1)} %get-tuple-element.2160, ...), kind=kOutput, calls=%fused_computation.89.clone.1 | convolution fusion | flops 811532288 | bytes 2851584 | tf_op jit(solution)/shard_map/jvp()/while/body/eval_jaxpr/mhts,shd->mhtd/dot_general | solution.py:94
  179.2 10.2 %multiply_reduce_fusion.11 = (f32[4,128,128]{1,2,0:T(8,128)S(1)}, f32[8,4,128,128]{3,2,0,1:T(8,128)S(1)}) fusion(f32[4,128,8]{1,2,0:T(8,128)S(1)} %copy.360, f32[8,4,128]{2,0,1:T(8,128)S(1)} %get-tuple-element.2160, f32[8,4,128]{2,0,1:T(8,128)S(1)} %bitcast.427, f32[8,4,128]{2,0,1:T(8,128)S(1)} %get-tuple-element.2161, ...), kind=kOutput, calls=%fused_computation.88.clone.1 | convolution fusion | flops 811532288 | bytes 2851584 | tf_op jit(solution)/shard_map/jvp()/while/body/eval_jaxpr/mhts,shd->mhtd/dot_general | solution.py:97
  189.4 10.3 %multiply_reduce_fusion.10 = (f32[4,128,128]{1,2,0:T(8,128)S(1)}, f32[8,4,128,128]{3,2,0,1:T(8,128)S(1)}) fusion(f32[4,128,8]{1,2,0:T(8,128)S(1)} %copy.359, f32[8,4,128]{2,0,1:T(8,128)S(1)} %get-tuple-element.2161, f32[8,4,128]{2,0,1:T(8,128)S(1)} %bitcast.428, f32[8,4,128]{2,0,1:T(8,128)S(1)} %get-tuple-element.2160, ...), kind=kOutput, calls=%fused_computation.89.clone.1 | convolution fusion | flops 811532288 | bytes 2851584 | tf_op jit(solution)/shard_map/jvp()/while/body/eval_jaxpr/mhts,shd->mhtd/dot_general | solution.py:94
  203.5 10.2 %multiply_reduce_fusion.11 = (f32[4,128,128]{1,2,0:T(8,128)S(1)}, f32[8,4,128,128]{3,2,0,1:T(8,128)S(1)}) fusion(f32[4,128,8]{1,2,0:T(8,128)S(1)} %copy.360, f32[8,4,128]{2,0,1:T(8,128)S(1)} %get-tuple-element.2160, f32[8,4,128]{2,0,1:T(8,128)S(1)} %bitcast.427, f32[8,4,128]{2,0,1:T(8,128)S(1)} %get-tuple-element.2161, ...), kind=kOutput, calls=%fused_computation.88.clone.1 | convolution fusion | flops 811532288 | bytes 2851584 | tf_op jit(solution)/shard_map/jvp()/while/body/eval_jaxpr/mhts,shd->mhtd/dot_general | solution.py:97
  213.7 10.3 %multiply_reduce_fusion.10 = (f32[4,128,128]{1,2,0:T(8,128)S(1)}, f32[8,4,128,128]{3,2,0,1:T(8,128)S(1)}) fusion(f32[4,128,8]{1,2,0:T(8,128)S(1)} %copy.359, f32[8,4,128]{2,0,1:T(8,128)S(1)} %get-tuple-element.2161, f32[8,4,128]{2,0,1:T(8,128)S(1)} %bitcast.428, f32[8,4,128]{2,0,1:T(8,128)S(1)} %get-tuple-element.2160, ...), kind=kOutput, calls=%fused_computation.89.clone.1 | convolution fusion | flops 811532288 | bytes 2851584 | tf_op jit(solution)/shard_map/jvp()/while/body/eval_jaxpr/mhts,shd->mhtd/dot_general | solution.py:94
  228.2 13.2 %all-gather.2 = f32[32,4,128]{2,0,1:T(8,128)S(1)} all-gather(f32[8,4,128]{2,0,1:T(8,128)S(1)} %get-tuple-element.821), channel_id=4, replica_groups=mesh['group'=2,'tm'=4,'tensor'=2,'dp'=2] {'tm'}, dimensions={0}, use_global_device_ids=true | all-gather | bytes 81920 | tf_op jit(solution)/shard_map/all_gather | solution.py:12
  241.4 13.2 %all-gather.3 = f32[32,4,128]{2,0,1:T(8,128)S(1)} all-gather(f32[8,4,128]{2,0,1:T(8,128)S(1)} %get-tuple-element.822), channel_id=5, replica_groups=mesh['group'=2,'tm'=4,'tensor'=2,'dp'=2] {'tm'}, dimensions={0}, use_global_device_ids=true | all-gather | bytes 81920 | tf_op jit(solution)/shard_map/all_gather | solution.py:12
  261.2 13.2 %all-gather.4 = f32[32,4,128]{2,0,1:T(8,128)S(1)} all-gather(f32[8,4,128]{2,0,1:T(8,128)S(1)} %get-tuple-element.1702), channel_id=6, replica_groups=mesh['group'=2,'tm'=4,'tensor'=2,'dp'=2] {'tm'}, dimensions={0}, use_global_device_ids=true | all-gather | bytes 81920 | tf_op jit(solution)/shard_map/all_gather | solution.py:12
  274.5 13.2 %all-gather.5 = f32[32,4,128]{2,0,1:T(8,128)S(1)} all-gather(f32[8,4,128]{2,0,1:T(8,128)S(1)} %get-tuple-element.1666), channel_id=7, replica_groups=mesh['group'=2,'tm'=4,'tensor'=2,'dp'=2] {'tm'}, dimensions={0}, use_global_device_ids=true | all-gather | bytes 81920 | tf_op jit(solution)/shard_map/all_gather | solution.py:12
  290.9 312.5 %while.83 = (s32[]{:T(128)}, f32[4,128]{1,0:T(4,128)S(1)}, f32[8,4,128]{2,1,0:T(4,128)}, f32[8,4,128]{2,1,0:T(4,128)}, f32[8,4,128]{2,0,1:T(8,128)}, /*index=5*/...) while((s32[]{:T(128)}, f32[4,128]{1,0:T(4,128)S(1)}, ...), condition=%wide.region_15.16_spmd.clone.clone.clone, body=%wide.region_9.15_spmd.clone.clone.clone.sunk | while | flops 3254166272 | bytes 45512152 | solution.py:124
  291.1 10.1 %fusion.192 = (f32[8,4,128,128]{3,2,0,1:T(8,128)}, f32[8,4,128,128]{3,2,0,1:T(8,128)}) fusion(f32[8,4]{0,1:T(4,128)S(1)} %get-tuple-element.2328, f32[128,128]{1,0:T(8,128)} %get-tuple-element.2327, f32[8,4]{0,1:T(4,128)S(1)} %get-tuple-element.2325, pred[128,128]{1,0:T(8,128)(4,1)S(1)} %get-tuple-element.2326), kind=kLoop, calls=%fused_computation.23.clone.1 | loop fusion | flops 2621440 | bytes 4276480 | tf_op jit(solution)/shard_map/mul | solution.py:57
  311.8 4.5 fusion.194
  320.6 4.5 fusion.195
  329.4 6.1 multiply_reduce_fusion.12
  343.2 10.1 %fusion.192 = (f32[8,4,128,128]{3,2,0,1:T(8,128)}, f32[8,4,128,128]{3,2,0,1:T(8,128)}) fusion(f32[8,4]{0,1:T(4,128)S(1)} %get-tuple-element.2328, f32[128,128]{1,0:T(8,128)} %get-tuple-element.2327, f32[8,4]{0,1:T(4,128)S(1)} %get-tuple-element.2325, pred[128,128]{1,0:T(8,128)(4,1)S(1)} %get-tuple-element.2326), kind=kLoop, calls=%fused_computation.23.clone.1 | loop fusion | flops 2621440 | bytes 4276480 | tf_op jit(solution)/shard_map/mul | solution.py:57
  372.6 4.5 fusion.195
  381.4 6.1 multiply_reduce_fusion.12
  395.2 10.1 %fusion.192 = (f32[8,4,128,128]{3,2,0,1:T(8,128)}, f32[8,4,128,128]{3,2,0,1:T(8,128)}) fusion(f32[8,4]{0,1:T(4,128)S(1)} %get-tuple-element.2328, f32[128,128]{1,0:T(8,128)} %get-tuple-element.2327, f32[8,4]{0,1:T(4,128)S(1)} %get-tuple-element.2325, pred[128,128]{1,0:T(8,128)(4,1)S(1)} %get-tuple-element.2326), kind=kLoop, calls=%fused_computation.23.clone.1 | loop fusion | flops 2621440 | bytes 4276480 | tf_op jit(solution)/shard_map/mul | solution.py:57
  424.7 4.5 fusion.195
  433.4 6.1 multiply_reduce_fusion.12
  447.2 10.1 %fusion.192 = (f32[8,4,128,128]{3,2,0,1:T(8,128)}, f32[8,4,128,128]{3,2,0,1:T(8,128)}) fusion(f32[8,4]{0,1:T(4,128)S(1)} %get-tuple-element.2328, f32[128,128]{1,0:T(8,128)} %get-tuple-element.2327, f32[8,4]{0,1:T(4,128)S(1)} %get-tuple-element.2325, pred[128,128]{1,0:T(8,128)(4,1)S(1)} %get-tuple-element.2326), kind=kLoop, calls=%fused_computation.23.clone.1 | loop fusion | flops 2621440 | bytes 4276480 | tf_op jit(solution)/shard_map/mul | solution.py:57
  467.8 4.5 fusion.194
  476.7 4.5 fusion.195
  485.4 6.1 multiply_reduce_fusion.12
  499.3 10.1 %fusion.192 = (f32[8,4,128,128]{3,2,0,1:T(8,128)}, f32[8,4,128,128]{3,2,0,1:T(8,128)}) fusion(f32[8,4]{0,1:T(4,128)S(1)} %get-tuple-element.2328, f32[128,128]{1,0:T(8,128)} %get-tuple-element.2327, f32[8,4]{0,1:T(4,128)S(1)} %get-tuple-element.2325, pred[128,128]{1,0:T(8,128)(4,1)S(1)} %get-tuple-element.2326), kind=kLoop, calls=%fused_computation.23.clone.1 | loop fusion | flops 2621440 | bytes 4276480 | tf_op jit(solution)/shard_map/mul | solution.py:57
  537.5 6.1 multiply_reduce_fusion.12
  551.3 10.1 %fusion.192 = (f32[8,4,128,128]{3,2,0,1:T(8,128)}, f32[8,4,128,128]{3,2,0,1:T(8,128)}) fusion(f32[8,4]{0,1:T(4,128)S(1)} %get-tuple-element.2328, f32[128,128]{1,0:T(8,128)} %get-tuple-element.2327, f32[8,4]{0,1:T(4,128)S(1)} %get-tuple-element.2325, pred[128,128]{1,0:T(8,128)(4,1)S(1)} %get-tuple-element.2326), kind=kLoop, calls=%fused_computation.23.clone.1 | loop fusion | flops 2621440 | bytes 4276480 | tf_op jit(solution)/shard_map/mul | solution.py:57
  571.9 4.5 fusion.194
  580.8 4.5 fusion.195
  589.5 6.1 multiply_reduce_fusion.12
  607.5 5.7 multiply_bitcast_fusion
  614.3 4.7 convolution_bitcast_fusion
  619.1 23.6 %all-reduce.11.cloned.1.call-done = f32[2,1024,512]{1,2,0:T(8,128)} async-done(((f32[2,1024,512]{1,2,0:T(8,128)}), f32[2,1024,512]{1,2,0:T(8,128)}) %all-reduce.11.cloned.1.call-update) | async-done | bytes 4194320 | tf_op jit(solution)/shard_map/psum | solution.py:184
  648.5 20.3 %all-reduce.6 = (f32[2,8,512]{2,1,0:T(8,128)}, f32[512]{0:T(512)}) all-reduce(f32[2,8,512]{2,1,0:T(8,128)S(1)} %get-tuple-element.1662, f32[512]{0:T(512)S(1)} %get-tuple-element.1663), channel_id=1, replica_groups=mesh['group'=2,'tm'=4,'tensor'=2,'dp'=2] {'tm'}, use_global_device_ids=true, to_apply=%region_20.21 | all-reduce | flops 8704 | bytes 69632 | tf_op jit(solution)/shard_map/psum | solution.py:183
  668.8 20.7 %reduce-scatter.2.cloned.1.call-done = f32[1,768,512]{2,1,0:T(8,128)} async-done(((f32[1,768,1024]{2,1,0:T(8,128)}), f32[1,768,512]{2,1,0:T(8,128)}) %reduce-scatter.2.cloned.1.call-update) | async-done | bytes 1572880 | tf_op jit(solution)/shard_map/reduce_scatter | solution.py:173
  691.9 154.8 %all-reduce.13.cloned.1.call-done = f32[2,1024,512]{1,2,0:T(8,128)} async-done(((f32[2,1024,512]{1,2,0:T(8,128)}), f32[2,1024,512]{1,2,0:T(8,128)}) %all-reduce.13.cloned.1.call-update) | async-done | bytes 4194320 | tf_op jit(solution)/shard_map/psum | solution.py:183
  846.8 5.4 copy.231
  (667 shorter events, 256.6 us)
Async XLA Ops:
  7.2 48.9 %copy-start = (bf16[2,1024,512]{2,1,0:T(8,128)(2,1)S(1)}, bf16[2,1024,512]{2,1,0:T(8,128)(2,1)}, u32[]{:S(2)}) copy-start(bf16[2,1024,512]{2,1,0:T(8,128)(2,1)} %param.17) | copy-start | bytes 6291460
  7.2 48.9 %all-gather.9.cloned.1.call-start = ((), (), s32[]{:S(2)}) async-start(), calls=%async_computation.1 | async-start | bytes 2359296 | tf_op jit(solution)/shard_map/all_gather | solution.py:45
  7.9 634.7 %all-reduce.11.cloned.1.call-start = ((), (), s32[]{:S(2)}) async-start(), calls=%async_computation.3 | async-start | bytes 8388608 | tf_op jit(solution)/shard_map/psum | solution.py:184
  11.8 248.7 %copy-start.38 = (f32[8,4]{0,1:T(4,128)}, f32[8,4]{0,1:T(4,128)S(1)}, u32[]{:S(2)}) copy-start(f32[8,4]{0,1:T(4,128)S(1)} %get-tuple-element.1707) | copy-start | bytes 388
  260.5 30.4 %copy-start.31 = (f32[4,128]{1,0:T(4,128)S(1)}, f32[4,128]{1,0:T(4,128)}, u32[]{:S(2)}) copy-start(f32[4,128]{1,0:T(4,128)} %custom-call.4) | copy-start | bytes 6148
  291.1 10.1 %copy-start.11 = (pred[128,128]{1,0:T(8,128)(4,1)}, pred[128,128]{1,0:T(8,128)(4,1)S(1)}, u32[]{:S(2)}) copy-start(pred[128,128]{1,0:T(8,128)(4,1)S(1)} %get-tuple-element.2326) | copy-start | bytes 49156 | tf_op jit(solution)/shard_map/transpose(jvp())/while
  291.1 10.1 %copy-start.21 = (f32[8,4]{0,1:T(4,128)}, f32[8,4]{0,1:T(4,128)S(1)}, u32[]{:S(2)}) copy-start(f32[8,4]{0,1:T(4,128)S(1)} %get-tuple-element.2325) | copy-start | bytes 388 | tf_op jit(solution)/shard_map/transpose(jvp())/while
  291.1 10.1 %copy-start.24 = (f32[8,4]{0,1:T(4,128)}, f32[8,4]{0,1:T(4,128)S(1)}, u32[]{:S(2)}) copy-start(f32[8,4]{0,1:T(4,128)S(1)} %get-tuple-element.2328) | copy-start | bytes 388 | tf_op jit(solution)/shard_map/transpose(jvp())/while
  291.1 10.1 %copy-start.27 = (f32[4,128]{1,0:T(4,128)}, f32[4,128]{1,0:T(4,128)S(1)}, u32[]{:S(2)}) copy-start(f32[4,128]{1,0:T(4,128)S(1)} %get-tuple-element.2139) | copy-start | bytes 6148 | tf_op jit(solution)/shard_map/transpose(jvp())/while
  291.1 12.7 %copy-start.40 = (s32[6,128]{1,0:T(8,128)}, s32[6,128]{1,0:T(8,128)S(1)}, u32[]{:S(2)}) copy-start(s32[6,128]{1,0:T(8,128)S(1)} %get-tuple-element.2317) | copy-start | bytes 9220 | tf_op jit(solution)/shard_map/transpose(jvp())/while
  291.1 12.7 %copy-start.45 = (s32[6]{0:T(128)}, s32[6]{0:T(128)S(1)}, u32[]{:S(2)}) copy-start(s32[6]{0:T(128)S(1)} %get-tuple-element.2318) | copy-start | bytes 76 | tf_op jit(solution)/shard_map/transpose(jvp())/while
  329.3 7.3 copy-start.1
  343.1 10.1 %copy-start.11 = (pred[128,128]{1,0:T(8,128)(4,1)}, pred[128,128]{1,0:T(8,128)(4,1)S(1)}, u32[]{:S(2)}) copy-start(pred[128,128]{1,0:T(8,128)(4,1)S(1)} %get-tuple-element.2326) | copy-start | bytes 49156 | tf_op jit(solution)/shard_map/transpose(jvp())/while
  343.1 10.1 %copy-start.21 = (f32[8,4]{0,1:T(4,128)}, f32[8,4]{0,1:T(4,128)S(1)}, u32[]{:S(2)}) copy-start(f32[8,4]{0,1:T(4,128)S(1)} %get-tuple-element.2325) | copy-start | bytes 388 | tf_op jit(solution)/shard_map/transpose(jvp())/while
  343.1 10.1 %copy-start.24 = (f32[8,4]{0,1:T(4,128)}, f32[8,4]{0,1:T(4,128)S(1)}, u32[]{:S(2)}) copy-start(f32[8,4]{0,1:T(4,128)S(1)} %get-tuple-element.2328) | copy-start | bytes 388 | tf_op jit(solution)/shard_map/transpose(jvp())/while
  343.1 10.1 %copy-start.27 = (f32[4,128]{1,0:T(4,128)}, f32[4,128]{1,0:T(4,128)S(1)}, u32[]{:S(2)}) copy-start(f32[4,128]{1,0:T(4,128)S(1)} %get-tuple-element.2139) | copy-start | bytes 6148 | tf_op jit(solution)/shard_map/transpose(jvp())/while
  343.1 12.7 %copy-start.40 = (s32[6,128]{1,0:T(8,128)}, s32[6,128]{1,0:T(8,128)S(1)}, u32[]{:S(2)}) copy-start(s32[6,128]{1,0:T(8,128)S(1)} %get-tuple-element.2317) | copy-start | bytes 9220 | tf_op jit(solution)/shard_map/transpose(jvp())/while
  343.2 12.7 %copy-start.45 = (s32[6]{0:T(128)}, s32[6]{0:T(128)S(1)}, u32[]{:S(2)}) copy-start(s32[6]{0:T(128)S(1)} %get-tuple-element.2318) | copy-start | bytes 76 | tf_op jit(solution)/shard_map/transpose(jvp())/while
  381.4 7.3 copy-start.1
  395.1 10.1 %copy-start.11 = (pred[128,128]{1,0:T(8,128)(4,1)}, pred[128,128]{1,0:T(8,128)(4,1)S(1)}, u32[]{:S(2)}) copy-start(pred[128,128]{1,0:T(8,128)(4,1)S(1)} %get-tuple-element.2326) | copy-start | bytes 49156 | tf_op jit(solution)/shard_map/transpose(jvp())/while
  395.2 10.1 %copy-start.21 = (f32[8,4]{0,1:T(4,128)}, f32[8,4]{0,1:T(4,128)S(1)}, u32[]{:S(2)}) copy-start(f32[8,4]{0,1:T(4,128)S(1)} %get-tuple-element.2325) | copy-start | bytes 388 | tf_op jit(solution)/shard_map/transpose(jvp())/while
  395.2 10.1 %copy-start.24 = (f32[8,4]{0,1:T(4,128)}, f32[8,4]{0,1:T(4,128)S(1)}, u32[]{:S(2)}) copy-start(f32[8,4]{0,1:T(4,128)S(1)} %get-tuple-element.2328) | copy-start | bytes 388 | tf_op jit(solution)/shard_map/transpose(jvp())/while
  395.2 10.1 %copy-start.27 = (f32[4,128]{1,0:T(4,128)}, f32[4,128]{1,0:T(4,128)S(1)}, u32[]{:S(2)}) copy-start(f32[4,128]{1,0:T(4,128)S(1)} %get-tuple-element.2139) | copy-start | bytes 6148 | tf_op jit(solution)/shard_map/transpose(jvp())/while
  395.2 12.7 %copy-start.40 = (s32[6,128]{1,0:T(8,128)}, s32[6,128]{1,0:T(8,128)S(1)}, u32[]{:S(2)}) copy-start(s32[6,128]{1,0:T(8,128)S(1)} %get-tuple-element.2317) | copy-start | bytes 9220 | tf_op jit(solution)/shard_map/transpose(jvp())/while
  395.2 12.7 %copy-start.45 = (s32[6]{0:T(128)}, s32[6]{0:T(128)S(1)}, u32[]{:S(2)}) copy-start(s32[6]{0:T(128)S(1)} %get-tuple-element.2318) | copy-start | bytes 76 | tf_op jit(solution)/shard_map/transpose(jvp())/while
  433.4 7.3 copy-start.1
  447.2 10.1 %copy-start.11 = (pred[128,128]{1,0:T(8,128)(4,1)}, pred[128,128]{1,0:T(8,128)(4,1)S(1)}, u32[]{:S(2)}) copy-start(pred[128,128]{1,0:T(8,128)(4,1)S(1)} %get-tuple-element.2326) | copy-start | bytes 49156 | tf_op jit(solution)/shard_map/transpose(jvp())/while
  447.2 10.1 %copy-start.21 = (f32[8,4]{0,1:T(4,128)}, f32[8,4]{0,1:T(4,128)S(1)}, u32[]{:S(2)}) copy-start(f32[8,4]{0,1:T(4,128)S(1)} %get-tuple-element.2325) | copy-start | bytes 388 | tf_op jit(solution)/shard_map/transpose(jvp())/while
  447.2 10.1 %copy-start.24 = (f32[8,4]{0,1:T(4,128)}, f32[8,4]{0,1:T(4,128)S(1)}, u32[]{:S(2)}) copy-start(f32[8,4]{0,1:T(4,128)S(1)} %get-tuple-element.2328) | copy-start | bytes 388 | tf_op jit(solution)/shard_map/transpose(jvp())/while
  447.2 10.1 %copy-start.27 = (f32[4,128]{1,0:T(4,128)}, f32[4,128]{1,0:T(4,128)S(1)}, u32[]{:S(2)}) copy-start(f32[4,128]{1,0:T(4,128)S(1)} %get-tuple-element.2139) | copy-start | bytes 6148 | tf_op jit(solution)/shard_map/transpose(jvp())/while
  447.2 12.7 %copy-start.40 = (s32[6,128]{1,0:T(8,128)}, s32[6,128]{1,0:T(8,128)S(1)}, u32[]{:S(2)}) copy-start(s32[6,128]{1,0:T(8,128)S(1)} %get-tuple-element.2317) | copy-start | bytes 9220 | tf_op jit(solution)/shard_map/transpose(jvp())/while
  447.2 12.7 %copy-start.45 = (s32[6]{0:T(128)}, s32[6]{0:T(128)S(1)}, u32[]{:S(2)}) copy-start(s32[6]{0:T(128)S(1)} %get-tuple-element.2318) | copy-start | bytes 76 | tf_op jit(solution)/shard_map/transpose(jvp())/while
  485.4 7.3 copy-start.1
  499.2 10.1 %copy-start.11 = (pred[128,128]{1,0:T(8,128)(4,1)}, pred[128,128]{1,0:T(8,128)(4,1)S(1)}, u32[]{:S(2)}) copy-start(pred[128,128]{1,0:T(8,128)(4,1)S(1)} %get-tuple-element.2326) | copy-start | bytes 49156 | tf_op jit(solution)/shard_map/transpose(jvp())/while
  499.2 10.1 %copy-start.21 = (f32[8,4]{0,1:T(4,128)}, f32[8,4]{0,1:T(4,128)S(1)}, u32[]{:S(2)}) copy-start(f32[8,4]{0,1:T(4,128)S(1)} %get-tuple-element.2325) | copy-start | bytes 388 | tf_op jit(solution)/shard_map/transpose(jvp())/while
  499.2 10.1 %copy-start.24 = (f32[8,4]{0,1:T(4,128)}, f32[8,4]{0,1:T(4,128)S(1)}, u32[]{:S(2)}) copy-start(f32[8,4]{0,1:T(4,128)S(1)} %get-tuple-element.2328) | copy-start | bytes 388 | tf_op jit(solution)/shard_map/transpose(jvp())/while
  499.2 10.1 %copy-start.27 = (f32[4,128]{1,0:T(4,128)}, f32[4,128]{1,0:T(4,128)S(1)}, u32[]{:S(2)}) copy-start(f32[4,128]{1,0:T(4,128)S(1)} %get-tuple-element.2139) | copy-start | bytes 6148 | tf_op jit(solution)/shard_map/transpose(jvp())/while
  499.2 12.7 %copy-start.40 = (s32[6,128]{1,0:T(8,128)}, s32[6,128]{1,0:T(8,128)S(1)}, u32[]{:S(2)}) copy-start(s32[6,128]{1,0:T(8,128)S(1)} %get-tuple-element.2317) | copy-start | bytes 9220 | tf_op jit(solution)/shard_map/transpose(jvp())/while
  499.2 12.7 %copy-start.45 = (s32[6]{0:T(128)}, s32[6]{0:T(128)S(1)}, u32[]{:S(2)}) copy-start(s32[6]{0:T(128)S(1)} %get-tuple-element.2318) | copy-start | bytes 76 | tf_op jit(solution)/shard_map/transpose(jvp())/while
  551.2 10.1 %copy-start.11 = (pred[128,128]{1,0:T(8,128)(4,1)}, pred[128,128]{1,0:T(8,128)(4,1)S(1)}, u32[]{:S(2)}) copy-start(pred[128,128]{1,0:T(8,128)(4,1)S(1)} %get-tuple-element.2326) | copy-start | bytes 49156 | tf_op jit(solution)/shard_map/transpose(jvp())/while
  551.2 10.1 %copy-start.21 = (f32[8,4]{0,1:T(4,128)}, f32[8,4]{0,1:T(4,128)S(1)}, u32[]{:S(2)}) copy-start(f32[8,4]{0,1:T(4,128)S(1)} %get-tuple-element.2325) | copy-start | bytes 388 | tf_op jit(solution)/shard_map/transpose(jvp())/while
  551.2 10.1 %copy-start.24 = (f32[8,4]{0,1:T(4,128)}, f32[8,4]{0,1:T(4,128)S(1)}, u32[]{:S(2)}) copy-start(f32[8,4]{0,1:T(4,128)S(1)} %get-tuple-element.2328) | copy-start | bytes 388 | tf_op jit(solution)/shard_map/transpose(jvp())/while
  551.2 10.1 %copy-start.27 = (f32[4,128]{1,0:T(4,128)}, f32[4,128]{1,0:T(4,128)S(1)}, u32[]{:S(2)}) copy-start(f32[4,128]{1,0:T(4,128)S(1)} %get-tuple-element.2139) | copy-start | bytes 6148 | tf_op jit(solution)/shard_map/transpose(jvp())/while
  551.3 12.7 %copy-start.40 = (s32[6,128]{1,0:T(8,128)}, s32[6,128]{1,0:T(8,128)S(1)}, u32[]{:S(2)}) copy-start(s32[6,128]{1,0:T(8,128)S(1)} %get-tuple-element.2317) | copy-start | bytes 9220 | tf_op jit(solution)/shard_map/transpose(jvp())/while
  551.3 12.7 %copy-start.45 = (s32[6]{0:T(128)}, s32[6]{0:T(128)S(1)}, u32[]{:S(2)}) copy-start(s32[6]{0:T(128)S(1)} %get-tuple-element.2318) | copy-start | bytes 76 | tf_op jit(solution)/shard_map/transpose(jvp())/while
  589.5 7.3 copy-start.1
  613.2 76.3 %reduce-scatter.2.cloned.1.call-start = ((), (), s32[]{:S(2)}) async-start(), calls=%async_computation.2 | async-start | bytes 4718592 | tf_op jit(solution)/shard_map/reduce_scatter | solution.py:173
  619.0 227.7 %all-reduce.13.cloned.1.call-start = ((), (), s32[]{:S(2)}) async-start(), calls=%async_computation.4 | async-start | bytes 8388608 | tf_op jit(solution)/shard_map/psum | solution.py:183
  (138 other events, 535.8 us)
Sparse Core Ops, SparseCore 0:
  9.6 29.8 all-gather.8
  613.3 29.2 all-reduce.10
  645.0 44.5 reduce-scatter.1
  691.7 154.9 all-reduce.12
